TPU v7x, 32 devices: a whole 2x2x4 slice. The times are simulated.
32 devices in a mesh: pipe: 2 (over core), expert: 16 (over z, y, x).
Axes of the slice: x: 2, y: 2, z: 4, core: 2. Of those that a mesh axis runs over, the one named last changes fastest.
Arguments:
- tokens: bfloat16 [4096, 2048], P(('pipe', 'expert')), may hold values from -6 to 6
- routes: int32 [4096, 8], P(('pipe', 'expert')), may hold values from 0 to 15, all different within a row; in each aligned block of 128 rows (0 to 127, 128 to 255, ...) at most 64 rows name the same one
- gates: float32 [4096, 8], P(('pipe', 'expert')), may hold values from 0.1 to 1
- cotangent: bfloat16 [4096, 2048], P(('pipe', 'expert')), may hold values from -1.5 to 1.5
- w_gate: bfloat16 [16, 2048, 384], P('expert'), may hold values from -0.125 to 0.125
- w_up: bfloat16 [16, 2048, 384], P('expert'), may hold values from -0.125 to 0.125
- w_down: bfloat16 [16, 384, 2048], P('expert'), may hold values from -0.3125 to 0.3125
Outputs:
- mixed: bfloat16 [4096, 2048], P(('pipe', 'expert'))
- input_grad: bfloat16 [4096, 2048], P(('pipe', 'expert'))
- gate_weight_grad: bfloat16 [16, 2048, 384], P('expert')
- up_weight_grad: bfloat16 [16, 2048, 384], P('expert')
- down_weight_grad: bfloat16 [16, 384, 2048], P('expert')
Inputs may be any that keep to these rules, and one draw needn't show every extreme that they name: `routes`: each row names 8 different experts. Within the rows of one device (aligned blocks of 128 rows, device order pipe then expert) each expert is named exactly 64 times.
All inputs are finite; a program needn't handle non-finite values.
Results may differ from a plain program's by a relative error of at most 0.009.
Values may be sent and summed in bfloat16 or wider, within the bound.
No kernel may reach another device: no remote copies, remote signals or barrier semaphores. Data moves between devices by JAX's collectives and lax.ppermute only.
A program may use at most 128 MiB of HBM per device.

v0:
```python
import jax
import jax.numpy as jnp
from jax import lax
from jax.sharding import PartitionSpec as P


def slot_index(block_routes, expert_count, capacity):
    flat = block_routes.reshape(-1)
    onehot = (flat[:, None] == jnp.arange(expert_count, dtype=jnp.int32)[None, :]).astype(jnp.int32)
    before = jnp.cumsum(onehot, axis=0) - onehot
    ranks = jnp.sum(before * onehot, axis=1)
    return flat * capacity + ranks


def expert_forward(block, gate_mat, up_mat, down_mat):
    inputs = block.reshape(-1, block.shape[2])
    gate_pre = jnp.dot(inputs, gate_mat, preferred_element_type=jnp.float32)
    up_pre = jnp.dot(inputs, up_mat, preferred_element_type=jnp.float32)
    sigma = jax.nn.sigmoid(gate_pre)
    hidden = (gate_pre * sigma * up_pre).astype(jnp.bfloat16)
    outputs = jnp.dot(hidden, down_mat, preferred_element_type=jnp.float32).astype(jnp.bfloat16)
    return (gate_pre, up_pre, hidden, outputs)


def on_device(tokens, routes, gates, cotangent, w_gate, w_up, w_down):
    rows_dev, width = tokens.shape
    picks = routes.shape[1]
    experts = lax.axis_size("expert")
    capacity = rows_dev * picks // experts
    gate_mat = w_gate[0]
    up_mat = w_up[0]
    down_mat = w_down[0]
    inner = gate_mat.shape[1]
    slots = slot_index(routes, experts, capacity)
    flat_rows = jnp.arange(rows_dev * picks, dtype=jnp.int32) // picks
    token_of = jnp.full((experts * capacity,), rows_dev, jnp.int32).at[slots].set(flat_rows)
    weight_of = jnp.zeros((experts * capacity,), jnp.float32).at[slots].set(gates.reshape(-1))
    token_pad = jnp.concatenate([tokens, jnp.zeros((1, width), tokens.dtype)], axis=0)
    send = token_pad[token_of].reshape(experts, capacity, width)
    block = lax.all_to_all(send, "expert", split_axis=0, concat_axis=0, tiled=True)
    items = block.shape[1]
    gate_pre, up_pre, hidden, outputs = expert_forward(block, gate_mat, up_mat, down_mat)
    back_items = lax.all_to_all(
        outputs.reshape(experts, items, width), "expert", split_axis=0, concat_axis=0, tiled=True
    )
    gate_three = gate_pre.reshape(experts, items, inner)
    up_three = up_pre.reshape(experts, items, inner)
    hidden_three = hidden.reshape(experts, items, inner)
    inputs = block.reshape(-1, width)
    gate_pre = gate_three.reshape(-1, inner)
    up_pre = up_three.reshape(-1, inner)
    hidden = hidden_three.reshape(-1, inner)
    gathered = back_items.reshape(-1, width)[slots].reshape(rows_dev, picks, width)
    mixed = jnp.sum(gates[:, :, None] * gathered.astype(jnp.float32), axis=1).astype(jnp.bfloat16)
    cot_pad = jnp.concatenate([cotangent, jnp.zeros((1, width), cotangent.dtype)], axis=0)
    cot_send = (weight_of[:, None] * cot_pad[token_of].astype(jnp.float32)).astype(jnp.bfloat16)
    slot_cot = lax.all_to_all(
        cot_send.reshape(experts, capacity, width),
        "expert",
        split_axis=0,
        concat_axis=0,
        tiled=True,
    ).reshape(-1, width)
    down_part = jnp.dot(hidden.T, slot_cot, preferred_element_type=jnp.float32)
    hidden_grad = jnp.dot(slot_cot, down_mat.T, preferred_element_type=jnp.float32)
    sigma = jax.nn.sigmoid(gate_pre)
    gate_grad = (hidden_grad * up_pre * sigma * (1.0 + gate_pre * (1.0 - sigma))).astype(
        jnp.bfloat16
    )
    up_grad = (hidden_grad * gate_pre * sigma).astype(jnp.bfloat16)
    slot_grads = (
        jnp.dot(gate_grad, gate_mat.T, preferred_element_type=jnp.float32)
        + jnp.dot(up_grad, up_mat.T, preferred_element_type=jnp.float32)
    ).astype(jnp.bfloat16)
    grads_back = lax.all_to_all(
        slot_grads.reshape(experts, capacity, width),
        "expert",
        split_axis=0,
        concat_axis=0,
        tiled=True,
    )
    gate_part = jnp.dot(inputs.T, gate_grad, preferred_element_type=jnp.float32)
    up_part = jnp.dot(inputs.T, up_grad, preferred_element_type=jnp.float32)
    gate_total, up_total, down_total = (
        lax.psum(gate_part.astype(jnp.bfloat16), "pipe").astype(jnp.float32),
        lax.psum(up_part.astype(jnp.bfloat16), "pipe").astype(jnp.float32),
        lax.psum(down_part.astype(jnp.bfloat16), "pipe").astype(jnp.float32),
    )
    grad_rows = grads_back.reshape(-1, width)[slots].reshape(rows_dev, picks, width)
    input_grad = jnp.sum(grad_rows.astype(jnp.float32), axis=1).astype(jnp.bfloat16)
    return (
        mixed,
        input_grad,
        gate_total.astype(jnp.bfloat16)[None],
        up_total.astype(jnp.bfloat16)[None],
        down_total.astype(jnp.bfloat16)[None],
    )


def solution(mesh):
    in_specs = (
        P(("pipe", "expert"), None),
        P(("pipe", "expert"), None),
        P(("pipe", "expert"), None),
        P(("pipe", "expert"), None),
        P("expert", None, None),
        P("expert", None, None),
        P("expert", None, None),
    )
    out_specs = (
        P(("pipe", "expert"), None),
        P(("pipe", "expert"), None),
        P("expert", None, None),
        P("expert", None, None),
        P("expert", None, None),
    )
    return jax.shard_map(
        on_device, mesh=mesh, in_specs=in_specs, out_specs=out_specs, check_vma=False
    )
```

profile of v0, /device:TPU:14, one launch (start us, length us, event | category | flops | bytes accessed | tf_op | source)
XLA Modules:
  0.0 467.3 jit_solution(10504910093243393587)
XLA Ops:
  7.2 0.8 broadcast_multiply_fusion
  9.2 4.5 reduce-window.6
  14.2 4.3 scatter_custom_fusion
  18.5 1.1 concatenate.6
  19.6 6.1 %gather_fusion = bf16[1024,2048]{1,0:T(8,128)(2,1)} fusion(bf16[129,2048]{1,0:T(8,128)(2,1)S(1)} %concatenate.6, s32[1024]{0:T(1024)S(1)} %fusion.21), kind=kCustom, calls=%fused_computation | custom fusion | bytes 8392704 | tf_op jit(solution)/shard_map/gather | solution.py:39
  25.7 7.3 %all-to-all-start = ((bf16[16,64,2048]{2,1,0:T(8,128)(2,1)}), bf16[16,64,2048]{2,1,0:T(8,128)(2,1)}, u32[]{:S(2)}, u32[]{:S(2)}) async-start(bf16[16,64,2048]{2,1,0:T(8,128)(2,1)} %bitcast.73), calls=%async_computation | async-start | bytes 8388608 | tf_op jit(solution)/shard_map/all_to_all | solution.py:40
  33.1 4.3 scatter_custom_fusion.1
  37.6 6.0 %gather_fusion.2 = bf16[1024,2048]{1,0:T(8,128)(2,1)} fusion(bf16[129,2048]{1,0:T(8,128)(2,1)S(1)} %concatenate.7, s32[1024]{0:T(1024)S(1)} %fusion.21), kind=kCustom, calls=%fused_computation.2 | custom fusion | bytes 8392704 | tf_op jit(solution)/shard_map/gather | solution.py:56
  43.6 4.9 %fusion = bf16[16,64,2048]{2,1,0:T(8,128)(2,1)} fusion(bf16[16,64,2048]{2,1,0:T(8,128)(2,1)} %bitcast.71, f32[16,64]{1,0:T(8,128)S(1)} %mul.70), kind=kLoop, calls=%fused_computation.7 | loop fusion | flops 6291456 | bytes 8392704 | tf_op jit(solution)/shard_map/convert_element_type | solution.py:56
  48.5 79.1 %all-to-all-done = bf16[16,64,2048]{2,1,0:T(8,128)(2,1)} async-done(((bf16[16,64,2048]{2,1,0:T(8,128)(2,1)}), bf16[16,64,2048]{2,1,0:T(8,128)(2,1)}, u32[]{:S(2)}, u32[]{:S(2)}) %all-to-all-start) | async-done | bytes 4194336 | tf_op jit(solution)/shard_map/all_to_all | solution.py:40
  127.6 5.1 %all-to-all-start.2 = ((bf16[16,64,2048]{2,1,0:T(8,128)(2,1)}), bf16[16,64,2048]{2,1,0:T(8,128)(2,1)}, u32[]{:S(2)}, u32[]{:S(2)}) async-start(bf16[16,64,2048]{2,1,0:T(8,128)(2,1)} %fusion), calls=%async_computation.2 | async-start | bytes 8388608 | tf_op jit(solution)/shard_map/all_to_all | solution.py:57
  132.7 6.2 %fusion.9 = f32[1024,384]{1,0:T(8,128)} fusion(bf16[1024,2048]{1,0:T(8,128)(2,1)} %bitcast.5, bf16[1,2048,384]{2,1,0:T(8,128)(2,1)} %param.12), kind=kOutput, calls=%fused_computation.23 | convolution fusion | flops 1610612736 | bytes 7340032 | tf_op jit(solution)/shard_map/dot_general | solution.py:18
  139.0 5.7 %fusion.13 = f32[1024,384]{1,0:T(8,128)} fusion(bf16[1024,2048]{1,0:T(8,128)(2,1)} %bitcast.5, bf16[1,2048,384]{2,1,0:T(8,128)(2,1)S(1)} %copy-done.3), kind=kOutput, calls=%fused_computation.27 | convolution fusion | flops 1610612736 | bytes 7340032 | tf_op jit(solution)/shard_map/dot_general | solution.py:17
  144.6 80.7 %all-to-all-done.2 = bf16[16,64,2048]{2,1,0:T(8,128)(2,1)} async-done(((bf16[16,64,2048]{2,1,0:T(8,128)(2,1)}), bf16[16,64,2048]{2,1,0:T(8,128)(2,1)}, u32[]{:S(2)}, u32[]{:S(2)}) %all-to-all-start.2) | async-done | bytes 4194336 | tf_op jit(solution)/shard_map/all_to_all | solution.py:57
  225.4 7.2 %multiply_convert_fusion = (bf16[1024,384]{1,0:T(8,128)(2,1)}, bf16[1024,384]{1,0:T(8,128)(2,1)}, bf16[1024,384]{1,0:T(8,128)(2,1)S(1)}) fusion(f32[1024,384]{1,0:T(8,128)} %fusion.13, f32[1024,384]{1,0:T(8,128)} %fusion.9, bf16[1024,2048]{1,0:T(8,128)(2,1)} %bitcast.13, bf16[1,384,2048]{2,1,0:T(8,128)(2,1)S(1)} %copy-done), kind=kOutput, calls=%fused_computation.29 | convolution fusion | flops 1616904192 | bytes 11272192 | tf_op jit(solution)/shard_map/dot_general | solution.py:65
  232.6 4.3 convolution_convert_fusion
  236.9 5.1 %all-to-all-start.1 = ((bf16[16,64,2048]{2,1,0:T(8,128)(2,1)}), bf16[16,64,2048]{2,1,0:T(8,128)(2,1)}, u32[]{:S(2)}, u32[]{:S(2)}) async-start(bf16[16,64,2048]{2,1,0:T(8,128)(2,1)} %bitcast.74), calls=%async_computation.1 | async-start | bytes 8388608 | tf_op jit(solution)/shard_map/all_to_all | solution.py:43
  242.0 3.6 fusion.11
  245.7 4.3 add_convert_fusion
  250.0 84.6 %all-to-all-done.1 = bf16[16,64,2048]{2,1,0:T(8,128)(2,1)} async-done(((bf16[16,64,2048]{2,1,0:T(8,128)(2,1)}), bf16[16,64,2048]{2,1,0:T(8,128)(2,1)}, u32[]{:S(2)}, u32[]{:S(2)}) %all-to-all-start.1) | async-done | bytes 4194336 | tf_op jit(solution)/shard_map/all_to_all | solution.py:43
  334.6 5.2 %all-to-all-start.3 = ((bf16[16,64,2048]{2,1,0:T(8,128)(2,1)}), bf16[16,64,2048]{2,1,0:T(8,128)(2,1)}, u32[]{:S(2)}, u32[]{:S(2)}) async-start(bf16[16,64,2048]{2,1,0:T(8,128)(2,1)} %bitcast.72), calls=%async_computation.3 | async-start | bytes 8388608 | tf_op jit(solution)/shard_map/all_to_all | solution.py:75
  339.9 5.2 %fusion.4 = bf16[1,384,2048]{2,1,0:T(8,128)(2,1)} fusion(bf16[1024,384]{1,0:T(8,128)(2,1)S(1)} %copy-done.13, bf16[1024,2048]{1,0:T(8,128)(2,1)} %bitcast.13), kind=kOutput, calls=%fused_computation.18 | convolution fusion | flops 1611399168 | bytes 6553600 | tf_op jit(solution)/shard_map/dot_general | solution.py:64
  345.2 5.8 %fusion.3 = bf16[1,2048,384]{2,1,0:T(8,128)(2,1)} fusion(bf16[1024,2048]{1,0:T(8,128)(2,1)} %bitcast.5, bf16[1024,384]{1,0:T(8,128)(2,1)S(1)} %copy-done.9), kind=kOutput, calls=%fused_computation.17 | convolution fusion | flops 1611399168 | bytes 6553600 | tf_op jit(solution)/shard_map/dot_general | solution.py:83
  351.0 5.7 %fusion.2 = bf16[1,2048,384]{2,1,0:T(8,128)(2,1)} fusion(bf16[1024,2048]{1,0:T(8,128)(2,1)} %bitcast.5, bf16[1024,384]{1,0:T(8,128)(2,1)S(1)} %copy-done.7), kind=kOutput, calls=%fused_computation.16 | convolution fusion | flops 1611399168 | bytes 6553600 | tf_op jit(solution)/shard_map/dot_general | solution.py:82
  356.7 11.8 %gather_fusion.1 = bf16[1024,2048]{1,0:T(8,128)(2,1)} fusion(bf16[1024,2048]{1,0:T(8,128)(2,1)} %bitcast.10, s32[1024]{0:T(1024)S(1)} %broadcast_clamp_fusion), kind=kCustom, calls=%fused_computation.1 | custom fusion | bytes 8392704 | tf_op jit(solution)/shard_map/gather | solution.py:53
  368.5 64.0 %all-to-all-done.3 = bf16[16,64,2048]{2,1,0:T(8,128)(2,1)} async-done(((bf16[16,64,2048]{2,1,0:T(8,128)(2,1)}), bf16[16,64,2048]{2,1,0:T(8,128)(2,1)}, u32[]{:S(2)}, u32[]{:S(2)}) %all-to-all-start.3) | async-done | bytes 4194336 | tf_op jit(solution)/shard_map/all_to_all | solution.py:75
  432.5 11.6 %gather_fusion.3 = bf16[1024,2048]{1,0:T(8,128)(2,1)} fusion(bf16[1024,2048]{1,0:T(8,128)(2,1)} %bitcast.15, s32[1024]{0:T(1024)S(1)} %broadcast_clamp_fusion), kind=kCustom, calls=%fused_computation.3 | custom fusion | bytes 8392704 | tf_op jit(solution)/shard_map/gather | solution.py:89
  444.1 6.0 %bitcast_reduce_fusion = bf16[128,2048]{1,0:T(8,128)(2,1)} fusion(bf16[1024,2048]{1,0:T(8,128)(2,1)} %gather_fusion.3), kind=kLoop, calls=%fused_computation.11 | loop fusion | flops 1835008 | bytes 4718592 | tf_op jit(solution)/shard_map/reduce_sum | solution.py:90
  450.1 5.2 %fusion.1 = bf16[128,2048]{1,0:T(8,128)(2,1)} fusion(bf16[1024,2048]{1,0:T(8,128)(2,1)S(1)} %copy-done.2, f32[128,8]{1,0:T(8,128)S(1)} %copy.15), kind=kLoop, calls=%fused_computation.9 | loop fusion | flops 6029312 | bytes 4722688 | tf_op jit(solution)/shard_map/reduce_sum | solution.py:54
  455.3 2.9 copy.27
  458.2 1.1 copy.28
  459.3 1.1 copy.29
  (52 shorter events, 2.1 us)
Async XLA Ops:
  7.2 218.2 %copy-start = (bf16[1,384,2048]{2,1,0:T(8,128)(2,1)S(1)}, bf16[1,384,2048]{2,1,0:T(8,128)(2,1)}, u32[]{:S(2)}) copy-start(bf16[1,384,2048]{2,1,0:T(8,128)(2,1)} %param.13) | copy-start | bytes 4718596
  25.7 7.3 %copy-start.11 = (f32[128,8]{0,1:T(8,128)S(1)}, f32[128,8]{0,1:T(8,128)}, u32[]{:S(2)}) copy-start(f32[128,8]{0,1:T(8,128)} %param.9) | copy-start | bytes 12292
  25.7 11.9 %copy-start.10 = (bf16[128,2048]{1,0:T(8,128)(2,1)S(1)}, bf16[128,2048]{1,0:T(8,128)(2,1)}, u32[]{:S(2)}) copy-start(bf16[128,2048]{1,0:T(8,128)(2,1)} %param.10) | copy-start | bytes 1572868
  25.7 101.9 %all-to-all-start = ((bf16[16,64,2048]{2,1,0:T(8,128)(2,1)}), bf16[16,64,2048]{2,1,0:T(8,128)(2,1)}, u32[]{:S(2)}, u32[]{:S(2)}) async-start(bf16[16,64,2048]{2,1,0:T(8,128)(2,1)} %bitcast.73), calls=%async_computation | async-start | bytes 8388608 | tf_op jit(solution)/shard_map/all_to_all | solution.py:40
  127.6 97.8 %all-to-all-start.2 = ((bf16[16,64,2048]{2,1,0:T(8,128)(2,1)}), bf16[16,64,2048]{2,1,0:T(8,128)(2,1)}, u32[]{:S(2)}, u32[]{:S(2)}) async-start(bf16[16,64,2048]{2,1,0:T(8,128)(2,1)} %fusion), calls=%async_computation.2 | async-start | bytes 8388608 | tf_op jit(solution)/shard_map/all_to_all | solution.py:57
  132.7 6.3 %copy-start.3 = (bf16[1,2048,384]{2,1,0:T(8,128)(2,1)S(1)}, bf16[1,2048,384]{2,1,0:T(8,128)(2,1)}, u32[]{:S(2)}) copy-start(bf16[1,2048,384]{2,1,0:T(8,128)(2,1)} %param.11) | copy-start | bytes 4718596
  232.6 4.3 copy-start.12
  236.9 97.8 %all-to-all-start.1 = ((bf16[16,64,2048]{2,1,0:T(8,128)(2,1)}), bf16[16,64,2048]{2,1,0:T(8,128)(2,1)}, u32[]{:S(2)}, u32[]{:S(2)}) async-start(bf16[16,64,2048]{2,1,0:T(8,128)(2,1)} %bitcast.74), calls=%async_computation.1 | async-start | bytes 8388608 | tf_op jit(solution)/shard_map/all_to_all | solution.py:43
  242.0 3.7 copy-start.4
  242.0 3.7 copy-start.8
  334.6 5.3 %copy-start.13 = (bf16[1024,384]{1,0:T(8,128)(2,1)S(1)}, bf16[1024,384]{1,0:T(8,128)(2,1)}, u32[]{:S(2)}) copy-start(bf16[1024,384]{1,0:T(8,128)(2,1)} %copy-done.12) | copy-start | bytes 2359300
  334.6 97.9 %all-to-all-start.3 = ((bf16[16,64,2048]{2,1,0:T(8,128)(2,1)}), bf16[16,64,2048]{2,1,0:T(8,128)(2,1)}, u32[]{:S(2)}, u32[]{:S(2)}) async-start(bf16[16,64,2048]{2,1,0:T(8,128)(2,1)} %bitcast.72), calls=%async_computation.3 | async-start | bytes 8388608 | tf_op jit(solution)/shard_map/all_to_all | solution.py:75
  339.9 5.3 %copy-start.9 = (bf16[1024,384]{1,0:T(8,128)(2,1)S(1)}, bf16[1024,384]{1,0:T(8,128)(2,1)}, u32[]{:S(2)}) copy-start(bf16[1024,384]{1,0:T(8,128)(2,1)} %get-tuple-element.8) | copy-start | bytes 2359300
  339.9 115.4 %all-reduce.5.cloned.1.call-start = ((), (), s32[]{:S(2)}) async-start(), calls=%async_computation.4 | async-start | bytes 9437184 | tf_op jit(solution)/shard_map/psum | solution.py:85
  345.2 5.8 %copy-start.7 = (bf16[1024,384]{1,0:T(8,128)(2,1)S(1)}, bf16[1024,384]{1,0:T(8,128)(2,1)}, u32[]{:S(2)}) copy-start(bf16[1024,384]{1,0:T(8,128)(2,1)} %get-tuple-element.9) | copy-start | bytes 2359300
  444.1 6.0 %copy-start.2 = (bf16[1024,2048]{1,0:T(8,128)(2,1)S(1)}, bf16[1024,2048]{1,0:T(8,128)(2,1)}, u32[]{:S(2)}) copy-start(bf16[1024,2048]{1,0:T(8,128)(2,1)} %gather_fusion.1) | copy-start | bytes 12582916
  455.3 2.9 copy-start.6
  455.3 4.0 copy-start.5
  455.3 5.2 %copy-start.1 = (bf16[1,384,2048]{2,1,0:T(8,128)(2,1)S(1)}, bf16[1,384,2048]{2,1,0:T(8,128)(2,1)}, u32[]{:S(2)}) copy-start(bf16[1,384,2048]{2,1,0:T(8,128)(2,1)} %param.13) | copy-start | bytes 4718596
Sparse Core Ops, SparseCore 0:
  356.8 30.5 all-reduce.4
where the time goes:
time: 468 us; the launch traced here: 467 us
  waiting for transfers between devices  309 us (66%)
  local copies, waits for them, and re-layouts  52.1 us (11%)
  matrix products  48.1 us (10%)
  starting transfers between devices  22.8 us (5%)
  other arithmetic  21.6 us (5%)
  between operations  14.2 us (3%)
    all_to_all x1, waiting for transfers between devices, on_device(): lax.all_to_all(outputs.reshape(experts, items, width), 'expert', split_ax...  84.6 us
    all_to_all x1, waiting for transfers between devices, on_device(): lax.all_to_all(cot_send.reshape(experts, capacity, width), 'expert', spli...  80.7 us
    all_to_all x1, waiting for transfers between devices, on_device(): lax.all_to_all(send, 'expert', split_axis=0, concat_axis=0, tiled=True)  79.1 us
    all_to_all x1, waiting for transfers between devices, on_device(): lax.all_to_all(slot_grads.reshape(experts, capacity, width), 'expert', sp...  64 us
    gather x1, local copies, waits for them, and re-layouts, on_device(): back_items.reshape(-1, width)[slots].reshape(rows_dev, picks, width)  11.8 us
    gather x1, local copies, waits for them, and re-layouts, on_device(): grads_back.reshape(-1, width)[slots].reshape(rows_dev, picks, width)  11.6 us
  transfers between devices with their start and end apart: 5, of which 4 were waited for; matrix products, arithmetic and copies ran while one was open for 19% of the time, Pallas kernels for 0%

commit v1 on v0

--- a/solution.py
+++ b/solution.py
@@ -2,6 +2,28 @@
 import jax.numpy as jnp
 from jax import lax
 from jax.sharding import PartitionSpec as P
+
+
+def cut_along(x, dim, peers):
+    before, after = (x.shape[:dim], x.shape[dim + 1 :])
+    return jnp.moveaxis(x.reshape(*before, peers, -1, *after), dim, 0)
+
+
+def laid_out(pieces, dim):
+    lengths = list(pieces.shape[1:])
+    lengths[dim] *= pieces.shape[0]
+    return jnp.moveaxis(pieces, 0, dim).reshape(lengths)
+
+
+def exchange_in_pairs(x, axis, split_dim, concat_dim):
+    size, index = (lax.axis_size(axis), lax.axis_index(axis))
+    tiles = cut_along(x, split_dim, size)
+    finished = [tiles[index]]
+    for step in range(1, size):
+        sent = tiles[index ^ step]
+        finished.append(lax.ppermute(sent, axis, [(i, i ^ step) for i in range(size)]))
+    tiles = jnp.stack(finished)[index ^ jnp.arange(size)]
+    return laid_out(tiles, concat_dim)
 
 
 def slot_index(block_routes, expert_count, capacity):
@@ -40,9 +62,7 @@
     block = lax.all_to_all(send, "expert", split_axis=0, concat_axis=0, tiled=True)
     items = block.shape[1]
     gate_pre, up_pre, hidden, outputs = expert_forward(block, gate_mat, up_mat, down_mat)
-    back_items = lax.all_to_all(
-        outputs.reshape(experts, items, width), "expert", split_axis=0, concat_axis=0, tiled=True
-    )
+    back_items = exchange_in_pairs(outputs.reshape(experts, items, width), "expert", 0, 0)
     gate_three = gate_pre.reshape(experts, items, inner)
     up_three = up_pre.reshape(experts, items, inner)
     hidden_three = hidden.reshape(experts, items, inner)

time: 468 us -> 527 us (1.13)
  the two profiles are of different devices: /device:TPU:14 before, /device:TPU:4 now
where the time goes in v1:
time: 527 us; the launch traced here: 526 us
  waiting for transfers between devices  311 us (59%)
  local copies, waits for them, and re-layouts  76.4 us (14%)
  starting transfers between devices  55 us (10%)
  matrix products  46 us (9%)
  other arithmetic  23.6 us (4%)
  between operations  14.2 us (3%)
    ppermute x15, waiting for transfers between devices, exchange_in_pairs(): lax.ppermute(sent, axis, [(i, i ^ step) for i in range(size)])  171 us
    all_to_all x1, waiting for transfers between devices, on_device(): lax.all_to_all(cot_send.reshape(experts, capacity, width), 'expert', spli...  70.9 us
    all_to_all x1, waiting for transfers between devices, on_device(): lax.all_to_all(send, 'expert', split_axis=0, concat_axis=0, tiled=True)  69.3 us
    unnamed x39, local copies, waits for them, and re-layouts  20.1 us
    ppermute x15, starting transfers between devices, exchange_in_pairs(): lax.ppermute(sent, axis, [(i, i ^ step) for i in range(size)])  17.7 us
    all_to_all x1, starting transfers between devices, on_device(): lax.all_to_all(slot_grads.reshape(experts, capacity, width), 'expert', sp...  14.9 us
    all_to_all x1, starting transfers between devices, on_device(): lax.all_to_all(cot_send.reshape(experts, capacity, width), 'expert', spli...  14.9 us
    gather x1, local copies, waits for them, and re-layouts, on_device(): back_items.reshape(-1, width)[slots].reshape(rows_dev, picks, width)  11.8 us
  transfers between devices with their start and end apart: 19, of which 13 were waited for; matrix products, arithmetic and copies ran while one was open for 18% of the time, Pallas kernels for 0%

profile of v1, /device:TPU:4, one launch (start us, length us, event | category | flops | bytes accessed | tf_op | source)
XLA Modules:
  0.0 526.0 jit_solution(8492351457403559349)
XLA Ops:
  9.2 4.5 reduce-window.6
  19.6 6.1 %gather_fusion = bf16[1024,2048]{1,0:T(8,128)(2,1)} fusion(bf16[129,2048]{1,0:T(8,128)(2,1)S(1)} %concatenate.6, s32[1024]{0:T(1024)S(1)} %fusion.21), kind=kCustom, calls=%fused_computation | custom fusion | bytes 8392704 | tf_op jit(solution)/shard_map/gather | solution.py:61
  25.7 7.4 %all-to-all-start = ((bf16[16,64,2048]{2,1,0:T(8,128)(2,1)}), bf16[16,64,2048]{2,1,0:T(8,128)(2,1)}, u32[]{:S(2)}, u32[]{:S(2)}) async-start(bf16[16,64,2048]{2,1,0:T(8,128)(2,1)} %bitcast.137), calls=%async_computation | async-start | bytes 8388608 | tf_op jit(solution)/shard_map/all_to_all | solution.py:62
  37.7 6.1 %gather_fusion.3 = bf16[1024,2048]{1,0:T(8,128)(2,1)} fusion(bf16[129,2048]{1,0:T(8,128)(2,1)S(1)} %concatenate.7, s32[1024]{0:T(1024)S(1)} %fusion.21), kind=kCustom, calls=%fused_computation.3 | custom fusion | bytes 8392704 | tf_op jit(solution)/shard_map/gather | solution.py:76
  43.8 4.9 fusion
  48.7 69.3 %all-to-all-done = bf16[16,64,2048]{2,1,0:T(8,128)(2,1)} async-done(((bf16[16,64,2048]{2,1,0:T(8,128)(2,1)}), bf16[16,64,2048]{2,1,0:T(8,128)(2,1)}, u32[]{:S(2)}, u32[]{:S(2)}) %all-to-all-start) | async-done | bytes 4194336 | tf_op jit(solution)/shard_map/all_to_all | solution.py:62
  118.0 14.9 %all-to-all-start.1 = ((bf16[16,64,2048]{2,1,0:T(8,128)(2,1)}), bf16[16,64,2048]{2,1,0:T(8,128)(2,1)}, u32[]{:S(2)}, u32[]{:S(2)}) async-start(bf16[16,64,2048]{2,1,0:T(8,128)(2,1)} %fusion), calls=%async_computation.1 | async-start | bytes 8388608 | tf_op jit(solution)/shard_map/all_to_all | solution.py:77
  132.9 6.3 %fusion.9 = f32[1024,384]{1,0:T(8,128)} fusion(bf16[1024,2048]{1,0:T(8,128)(2,1)} %bitcast.5, bf16[1,2048,384]{2,1,0:T(8,128)(2,1)} %param.12), kind=kOutput, calls=%fused_computation.24 | convolution fusion | flops 1610612736 | bytes 7340032 | tf_op jit(solution)/shard_map/dot_general | solution.py:40
  139.2 5.7 %fusion.13 = f32[1024,384]{1,0:T(8,128)} fusion(bf16[1024,2048]{1,0:T(8,128)(2,1)} %bitcast.5, bf16[1,2048,384]{2,1,0:T(8,128)(2,1)S(1)} %copy-done.2), kind=kOutput, calls=%fused_computation.28 | convolution fusion | flops 1610612736 | bytes 7340032 | tf_op jit(solution)/shard_map/dot_general | solution.py:39
  144.8 70.9 %all-to-all-done.1 = bf16[16,64,2048]{2,1,0:T(8,128)(2,1)} async-done(((bf16[16,64,2048]{2,1,0:T(8,128)(2,1)}), bf16[16,64,2048]{2,1,0:T(8,128)(2,1)}, u32[]{:S(2)}, u32[]{:S(2)}) %all-to-all-start.1) | async-done | bytes 4194336 | tf_op jit(solution)/shard_map/all_to_all | solution.py:77
  215.7 6.0 %multiply_convert_fusion = (bf16[1024,384]{1,0:T(8,128)(2,1)S(1)}, bf16[1024,384]{1,0:T(8,128)(2,1)S(1)}, bf16[1024,384]{1,0:T(8,128)(2,1)S(1)}) fusion(f32[1024,384]{1,0:T(8,128)} %fusion.13, f32[1024,384]{1,0:T(8,128)} %fusion.9, bf16[1024,2048]{1,0:T(8,128)(2,1)} %bitcast.45, bf16[1,384,2048]{2,1,0:T(8,128)(2,1)S(1)} %copy-done), kind=kOutput, calls=%fused_computation.30 | convolution fusion | flops 1616904192 | bytes 11272192 | tf_op jit(solution)/shard_map/dot_general | solution.py:85
  221.7 6.0 %fusion.2 = bf16[1,2048,384]{2,1,0:T(8,128)(2,1)} fusion(bf16[1024,2048]{1,0:T(8,128)(2,1)} %bitcast.5, bf16[1024,384]{1,0:T(8,128)(2,1)S(1)} %get-tuple-element.25), kind=kOutput, calls=%fused_computation.17 | convolution fusion | flops 1611399168 | bytes 6553600 | tf_op jit(solution)/shard_map/dot_general | solution.py:102
  230.1 5.7 %fusion.3 = bf16[1,2048,384]{2,1,0:T(8,128)(2,1)} fusion(bf16[1024,2048]{1,0:T(8,128)(2,1)} %bitcast.5, bf16[1024,384]{1,0:T(8,128)(2,1)S(1)} %get-tuple-element.24), kind=kOutput, calls=%fused_computation.18 | convolution fusion | flops 1611399168 | bytes 6553600 | tf_op jit(solution)/shard_map/dot_general | solution.py:103
  235.8 4.5 convolution_convert_fusion
  244.7 14.9 %all-to-all-start.2 = ((bf16[16,64,2048]{2,1,0:T(8,128)(2,1)}), bf16[16,64,2048]{2,1,0:T(8,128)(2,1)}, u32[]{:S(2)}, u32[]{:S(2)}) async-start(bf16[16,64,2048]{2,1,0:T(8,128)(2,1)} %bitcast.136), calls=%async_computation.2 | async-start | bytes 8388608 | tf_op jit(solution)/shard_map/all_to_all | solution.py:95
  274.1 5.2 fusion.4
  281.6 9.1 %collective-permute-done.1 = bf16[1,64,2048]{2,1,0:T(8,128)(2,1)S(1)} collective-permute-done((bf16[1,64,2048]{2,1,0:T(8,128)(2,1)}, bf16[1,64,2048]{2,1,0:T(8,128)(2,1)S(1)}, u32[]{:S(2)}, u32[]{:S(2)}) %collective-permute-start.1) | collective-permute-done | bytes 262176 | tf_op jit(solution)/shard_map/ppermute | solution.py:24
  292.0 29.5 %collective-permute-done.2 = bf16[1,64,2048]{2,1,0:T(8,128)(2,1)S(1)} collective-permute-done((bf16[1,64,2048]{2,1,0:T(8,128)(2,1)S(1)}, bf16[1,64,2048]{2,1,0:T(8,128)(2,1)S(1)}, u32[]{:S(2)}, u32[]{:S(2)}) %collective-permute-start.2) | collective-permute-done | bytes 262176 | tf_op jit(solution)/shard_map/ppermute | solution.py:24
  322.3 47.0 %collective-permute-done.3 = bf16[1,64,2048]{2,1,0:T(8,128)(2,1)S(1)} collective-permute-done((bf16[1,64,2048]{2,1,0:T(8,128)(2,1)S(1)}, bf16[1,64,2048]{2,1,0:T(8,128)(2,1)S(1)}, u32[]{:S(2)}, u32[]{:S(2)}) %collective-permute-start.3) | collective-permute-done | bytes 262176 | tf_op jit(solution)/shard_map/ppermute | solution.py:24
  370.0 7.2 %collective-permute-done.4 = bf16[1,64,2048]{2,1,0:T(8,128)(2,1)S(1)} collective-permute-done((bf16[1,64,2048]{2,1,0:T(8,128)(2,1)S(1)}, bf16[1,64,2048]{2,1,0:T(8,128)(2,1)S(1)}, u32[]{:S(2)}, u32[]{:S(2)}) %collective-permute-start.4) | collective-permute-done | bytes 262176 | tf_op jit(solution)/shard_map/ppermute | solution.py:24
  377.9 9.7 %collective-permute-done.5 = bf16[1,64,2048]{2,1,0:T(8,128)(2,1)S(1)} collective-permute-done((bf16[1,64,2048]{2,1,0:T(8,128)(2,1)S(1)}, bf16[1,64,2048]{2,1,0:T(8,128)(2,1)S(1)}, u32[]{:S(2)}, u32[]{:S(2)}) %collective-permute-start.5) | collective-permute-done | bytes 262176 | tf_op jit(solution)/shard_map/ppermute | solution.py:24
  388.4 7.4 %collective-permute-done.6 = bf16[1,64,2048]{2,1,0:T(8,128)(2,1)S(1)} collective-permute-done((bf16[1,64,2048]{2,1,0:T(8,128)(2,1)S(1)}, bf16[1,64,2048]{2,1,0:T(8,128)(2,1)S(1)}, u32[]{:S(2)}, u32[]{:S(2)}) %collective-permute-start.6) | collective-permute-done | bytes 262176 | tf_op jit(solution)/shard_map/ppermute | solution.py:24
  395.8 5.0 collective-permute-start.7
  401.5 32.0 %collective-permute-done.7 = bf16[1,64,2048]{2,1,0:T(8,128)(2,1)S(1)} collective-permute-done((bf16[1,64,2048]{2,1,0:T(8,128)(2,1)S(1)}, bf16[1,64,2048]{2,1,0:T(8,128)(2,1)S(1)}, u32[]{:S(2)}, u32[]{:S(2)}) %collective-permute-start.7) | collective-permute-done | bytes 262176 | tf_op jit(solution)/shard_map/ppermute | solution.py:24
  434.2 10.7 %collective-permute-done.8 = bf16[1,64,2048]{2,1,0:T(8,128)(2,1)S(1)} collective-permute-done((bf16[1,64,2048]{2,1,0:T(8,128)(2,1)S(1)}, bf16[1,64,2048]{2,1,0:T(8,128)(2,1)S(1)}, u32[]{:S(2)}, u32[]{:S(2)}) %collective-permute-start.8) | collective-permute-done | bytes 262176 | tf_op jit(solution)/shard_map/ppermute | solution.py:24
  445.7 9.3 %collective-permute-done.9 = bf16[1,64,2048]{2,1,0:T(8,128)(2,1)S(1)} collective-permute-done((bf16[1,64,2048]{2,1,0:T(8,128)(2,1)S(1)}, bf16[1,64,2048]{2,1,0:T(8,128)(2,1)S(1)}, u32[]{:S(2)}, u32[]{:S(2)}) %collective-permute-start.9) | collective-permute-done | bytes 262176 | tf_op jit(solution)/shard_map/ppermute | solution.py:24
  456.7 8.4 %collective-permute-done.10 = bf16[1,64,2048]{2,1,0:T(8,128)(2,1)S(1)} collective-permute-done((bf16[1,64,2048]{2,1,0:T(8,128)(2,1)S(1)}, bf16[1,64,2048]{2,1,0:T(8,128)(2,1)S(1)}, u32[]{:S(2)}, u32[]{:S(2)}) %collective-permute-start.10) | collective-permute-done | bytes 262176 | tf_op jit(solution)/shard_map/ppermute | solution.py:24
  472.5 5.0 gather_fusion.1
  477.4 11.8 %gather_fusion.2 = bf16[1024,2048]{1,0:T(8,128)(2,1)} fusion(bf16[1024,2048]{1,0:T(8,128)(2,1)} %bitcast.134, s32[1024]{0:T(1024)S(1)} %broadcast_clamp_fusion), kind=kCustom, calls=%fused_computation.2 | custom fusion | bytes 8392704 | tf_op jit(solution)/shard_map/gather | solution.py:73
  489.2 7.3 %fusion.1 = bf16[128,2048]{1,0:T(8,128)(2,1)} fusion(bf16[1024,2048]{1,0:T(8,128)(2,1)} %gather_fusion.2, f32[128,8]{1,0:T(8,128)S(1)} %copy.15), kind=kLoop, calls=%fused_computation.10 | loop fusion | flops 6029312 | bytes 4722688 | tf_op jit(solution)/shard_map/reduce_sum | solution.py:74
  496.6 11.6 %gather_fusion.4 = bf16[1024,2048]{1,0:T(8,128)(2,1)} fusion(bf16[1024,2048]{1,0:T(8,128)(2,1)} %bitcast.47, s32[1024]{0:T(1024)S(1)} %broadcast_clamp_fusion), kind=kCustom, calls=%fused_computation.4 | custom fusion | bytes 8392704 | tf_op jit(solution)/shard_map/gather | solution.py:109
  508.2 5.9 %bitcast_reduce_fusion = bf16[128,2048]{1,0:T(8,128)(2,1)} fusion(bf16[1024,2048]{1,0:T(8,128)(2,1)} %gather_fusion.4), kind=kLoop, calls=%fused_computation.12 | loop fusion | flops 1835008 | bytes 4718592 | tf_op jit(solution)/shard_map/reduce_sum | solution.py:110
  (91 shorter events, 56.7 us)
Async XLA Ops:
  7.2 208.6 %copy-start = (bf16[1,384,2048]{2,1,0:T(8,128)(2,1)S(1)}, bf16[1,384,2048]{2,1,0:T(8,128)(2,1)}, u32[]{:S(2)}) copy-start(bf16[1,384,2048]{2,1,0:T(8,128)(2,1)} %param.13) | copy-start | bytes 4718596
  25.7 7.4 %copy-start.7 = (f32[128,8]{0,1:T(8,128)S(1)}, f32[128,8]{0,1:T(8,128)}, u32[]{:S(2)}) copy-start(f32[128,8]{0,1:T(8,128)} %param.9) | copy-start | bytes 12292
  25.7 12.0 %copy-start.6 = (bf16[128,2048]{1,0:T(8,128)(2,1)S(1)}, bf16[128,2048]{1,0:T(8,128)(2,1)}, u32[]{:S(2)}) copy-start(bf16[128,2048]{1,0:T(8,128)(2,1)} %param.10) | copy-start | bytes 1572868
  25.7 92.3 %all-to-all-start = ((bf16[16,64,2048]{2,1,0:T(8,128)(2,1)}), bf16[16,64,2048]{2,1,0:T(8,128)(2,1)}, u32[]{:S(2)}, u32[]{:S(2)}) async-start(bf16[16,64,2048]{2,1,0:T(8,128)(2,1)} %bitcast.137), calls=%async_computation | async-start | bytes 8388608 | tf_op jit(solution)/shard_map/all_to_all | solution.py:62
  118.0 97.7 %all-to-all-start.1 = ((bf16[16,64,2048]{2,1,0:T(8,128)(2,1)}), bf16[16,64,2048]{2,1,0:T(8,128)(2,1)}, u32[]{:S(2)}, u32[]{:S(2)}) async-start(bf16[16,64,2048]{2,1,0:T(8,128)(2,1)} %fusion), calls=%async_computation.1 | async-start | bytes 8388608 | tf_op jit(solution)/shard_map/all_to_all | solution.py:77
  132.9 6.3 %copy-start.2 = (bf16[1,2048,384]{2,1,0:T(8,128)(2,1)S(1)}, bf16[1,2048,384]{2,1,0:T(8,128)(2,1)}, u32[]{:S(2)}) copy-start(bf16[1,2048,384]{2,1,0:T(8,128)(2,1)} %param.11) | copy-start | bytes 4718596
  221.7 14.1 %copy-start.8 = (bf16[1024,384]{1,0:T(8,128)(2,1)}, bf16[1024,384]{1,0:T(8,128)(2,1)S(1)}, u32[]{:S(2)}) copy-start(bf16[1024,384]{1,0:T(8,128)(2,1)S(1)} %get-tuple-element.26) | copy-start | bytes 2359300
  235.8 4.5 copy-start.3
  244.7 251.9 %all-to-all-start.2 = ((bf16[16,64,2048]{2,1,0:T(8,128)(2,1)}), bf16[16,64,2048]{2,1,0:T(8,128)(2,1)}, u32[]{:S(2)}, u32[]{:S(2)}) async-start(bf16[16,64,2048]{2,1,0:T(8,128)(2,1)} %bitcast.136), calls=%async_computation.2 | async-start | bytes 8388608 | tf_op jit(solution)/shard_map/all_to_all | solution.py:95
  259.6 254.4 %all-reduce.5.cloned.1.call-start = ((), (), s32[]{:S(2)}) async-start(), calls=%async_computation.3 | async-start | bytes 9437184 | tf_op jit(solution)/shard_map/psum | solution.py:105
  259.7 14.4 %copy-start.9 = (bf16[1024,384]{1,0:T(8,128)(2,1)S(1)}, bf16[1024,384]{1,0:T(8,128)(2,1)}, u32[]{:S(2)}) copy-start(bf16[1024,384]{1,0:T(8,128)(2,1)} %copy-done.8) | copy-start | bytes 2359300
  263.2 207.6 %collective-permute-start.14 = (bf16[1,64,2048]{2,1,0:T(8,128)(2,1)S(1)}, bf16[1,64,2048]{2,1,0:T(8,128)(2,1)}, u32[]{:S(2)}, u32[]{:S(2)}) collective-permute-start(bf16[1,64,2048]{2,1,0:T(8,128)(2,1)S(1)} %get-tuple-element.8), channel_id=1, source_target_pairs={{0,15},{1,14},{2,13},{3,12},{4,11},{5,10},{6,9},{7,8},{8,7},{9,6},... | collective-permute-start | bytes 786440 | tf_op jit(solution)/shard_map/ppermute | solution.py:24
  267.4 201.7 %collective-permute-start.13 = (bf16[1,64,2048]{2,1,0:T(8,128)(2,1)S(1)}, bf16[1,64,2048]{2,1,0:T(8,128)(2,1)}, u32[]{:S(2)}, u32[]{:S(2)}) collective-permute-start(bf16[1,64,2048]{2,1,0:T(8,128)(2,1)S(1)} %get-tuple-element.9), channel_id=1, source_target_pairs={{0,14},{1,15},{2,12},{3,13},{4,10},{5,11},{6,8},{7,9},{8,6},{9,7},... | collective-permute-start | bytes 786440 | tf_op jit(solution)/shard_map/ppermute | solution.py:24
  268.8 198.6 %collective-permute-start.12 = (bf16[1,64,2048]{2,1,0:T(8,128)(2,1)S(1)}, bf16[1,64,2048]{2,1,0:T(8,128)(2,1)}, u32[]{:S(2)}, u32[]{:S(2)}) collective-permute-start(bf16[1,64,2048]{2,1,0:T(8,128)(2,1)S(1)} %get-tuple-element.10), channel_id=1, source_target_pairs={{0,13},{1,12},{2,15},{3,14},{4,9},{5,8},{6,11},{7,10},{8,5},{9,4},... | collective-permute-start | bytes 786440 | tf_op jit(solution)/shard_map/ppermute | solution.py:24
  272.1 193.7 %collective-permute-start.11 = (bf16[1,64,2048]{2,1,0:T(8,128)(2,1)S(1)}, bf16[1,64,2048]{2,1,0:T(8,128)(2,1)}, u32[]{:S(2)}, u32[]{:S(2)}) collective-permute-start(bf16[1,64,2048]{2,1,0:T(8,128)(2,1)S(1)} %get-tuple-element.11), channel_id=1, source_target_pairs={{0,12},{1,13},{2,14},{3,15},{4,8},{5,9},{6,10},{7,11},{8,4},{9,5},... | collective-permute-start | bytes 786440 | tf_op jit(solution)/shard_map/ppermute | solution.py:24
  272.6 7.0 %collective-permute-start = (bf16[1,64,2048]{2,1,0:T(8,128)(2,1)}, bf16[1,64,2048]{2,1,0:T(8,128)(2,1)}, u32[]{:S(2)}, u32[]{:S(2)}) collective-permute-start(bf16[1,64,2048]{2,1,0:T(8,128)(2,1)} %get-tuple-element.22), channel_id=1, source_target_pairs={{0,1},{1,0},{2,3},{3,2},{4,5},{5,4},{6,7},{7,6},{8,9},{9,8},{10,11... | collective-permute-start | bytes 786440 | tf_op jit(solution)/shard_map/ppermute | solution.py:24
  279.7 11.0 %collective-permute-start.1 = (bf16[1,64,2048]{2,1,0:T(8,128)(2,1)}, bf16[1,64,2048]{2,1,0:T(8,128)(2,1)S(1)}, u32[]{:S(2)}, u32[]{:S(2)}) collective-permute-start(bf16[1,64,2048]{2,1,0:T(8,128)(2,1)} %get-tuple-element.21), channel_id=1, source_target_pairs={{0,2},{1,3},{2,0},{3,1},{4,6},{5,7},{6,4},{7,5},{8,10},{9,11},{10,... | collective-permute-start | bytes 786440 | tf_op jit(solution)/shard_map/ppermute | solution.py:24
  290.7 30.8 %collective-permute-start.2 = (bf16[1,64,2048]{2,1,0:T(8,128)(2,1)S(1)}, bf16[1,64,2048]{2,1,0:T(8,128)(2,1)S(1)}, u32[]{:S(2)}, u32[]{:S(2)}) collective-permute-start(bf16[1,64,2048]{2,1,0:T(8,128)(2,1)S(1)} %get-tuple-element.20), channel_id=1, source_target_pairs={{0,3},{1,2},{2,1},{3,0},{4,7},{5,6},{6,5},{7,4},{8,11},{9,10},{10,... | collective-permute-start | bytes 786440 | tf_op jit(solution)/shard_map/ppermute | solution.py:24
  321.5 47.7 %collective-permute-start.3 = (bf16[1,64,2048]{2,1,0:T(8,128)(2,1)S(1)}, bf16[1,64,2048]{2,1,0:T(8,128)(2,1)S(1)}, u32[]{:S(2)}, u32[]{:S(2)}) collective-permute-start(bf16[1,64,2048]{2,1,0:T(8,128)(2,1)S(1)} %get-tuple-element.19), channel_id=1, source_target_pairs={{0,4},{1,5},{2,6},{3,7},{4,0},{5,1},{6,2},{7,3},{8,12},{9,13},{10,... | collective-permute-start | bytes 786440 | tf_op jit(solution)/shard_map/ppermute | solution.py:24
  369.2 7.9 %collective-permute-start.4 = (bf16[1,64,2048]{2,1,0:T(8,128)(2,1)S(1)}, bf16[1,64,2048]{2,1,0:T(8,128)(2,1)S(1)}, u32[]{:S(2)}, u32[]{:S(2)}) collective-permute-start(bf16[1,64,2048]{2,1,0:T(8,128)(2,1)S(1)} %get-tuple-element.18), channel_id=1, source_target_pairs={{0,5},{1,4},{2,7},{3,6},{4,1},{5,0},{6,3},{7,2},{8,13},{9,12},{10,... | collective-permute-start | bytes 786440 | tf_op jit(solution)/shard_map/ppermute | solution.py:24
  377.1 10.5 %collective-permute-start.5 = (bf16[1,64,2048]{2,1,0:T(8,128)(2,1)S(1)}, bf16[1,64,2048]{2,1,0:T(8,128)(2,1)S(1)}, u32[]{:S(2)}, u32[]{:S(2)}) collective-permute-start(bf16[1,64,2048]{2,1,0:T(8,128)(2,1)S(1)} %get-tuple-element.17), channel_id=1, source_target_pairs={{0,6},{1,7},{2,4},{3,5},{4,2},{5,3},{6,0},{7,1},{8,14},{9,15},{10,... | collective-permute-start | bytes 786440 | tf_op jit(solution)/shard_map/ppermute | solution.py:24
  387.6 8.2 %collective-permute-start.6 = (bf16[1,64,2048]{2,1,0:T(8,128)(2,1)S(1)}, bf16[1,64,2048]{2,1,0:T(8,128)(2,1)S(1)}, u32[]{:S(2)}, u32[]{:S(2)}) collective-permute-start(bf16[1,64,2048]{2,1,0:T(8,128)(2,1)S(1)} %get-tuple-element.16), channel_id=1, source_target_pairs={{0,7},{1,6},{2,5},{3,4},{4,3},{5,2},{6,1},{7,0},{8,15},{9,14},{10,... | collective-permute-start | bytes 786440 | tf_op jit(solution)/shard_map/ppermute | solution.py:24
  395.8 37.7 %collective-permute-start.7 = (bf16[1,64,2048]{2,1,0:T(8,128)(2,1)S(1)}, bf16[1,64,2048]{2,1,0:T(8,128)(2,1)S(1)}, u32[]{:S(2)}, u32[]{:S(2)}) collective-permute-start(bf16[1,64,2048]{2,1,0:T(8,128)(2,1)S(1)} %get-tuple-element.15), channel_id=1, source_target_pairs={{0,8},{1,9},{2,10},{3,11},{4,12},{5,13},{6,14},{7,15},{8,0},{9,1},... | collective-permute-start | bytes 786440 | tf_op jit(solution)/shard_map/ppermute | solution.py:24
  433.5 11.5 %collective-permute-start.8 = (bf16[1,64,2048]{2,1,0:T(8,128)(2,1)S(1)}, bf16[1,64,2048]{2,1,0:T(8,128)(2,1)S(1)}, u32[]{:S(2)}, u32[]{:S(2)}) collective-permute-start(bf16[1,64,2048]{2,1,0:T(8,128)(2,1)S(1)} %get-tuple-element.14), channel_id=1, source_target_pairs={{0,9},{1,8},{2,11},{3,10},{4,13},{5,12},{6,15},{7,14},{8,1},{9,0},... | collective-permute-start | bytes 786440 | tf_op jit(solution)/shard_map/ppermute | solution.py:24
  444.9 10.0 %collective-permute-start.9 = (bf16[1,64,2048]{2,1,0:T(8,128)(2,1)S(1)}, bf16[1,64,2048]{2,1,0:T(8,128)(2,1)S(1)}, u32[]{:S(2)}, u32[]{:S(2)}) collective-permute-start(bf16[1,64,2048]{2,1,0:T(8,128)(2,1)S(1)} %get-tuple-element.13), channel_id=1, source_target_pairs={{0,10},{1,11},{2,8},{3,9},{4,14},{5,15},{6,12},{7,13},{8,2},{9,3},... | collective-permute-start | bytes 786440 | tf_op jit(solution)/shard_map/ppermute | solution.py:24
  455.0 10.1 %collective-permute-start.10 = (bf16[1,64,2048]{2,1,0:T(8,128)(2,1)S(1)}, bf16[1,64,2048]{2,1,0:T(8,128)(2,1)S(1)}, u32[]{:S(2)}, u32[]{:S(2)}) collective-permute-start(bf16[1,64,2048]{2,1,0:T(8,128)(2,1)S(1)} %get-tuple-element.12), channel_id=1, source_target_pairs={{0,11},{1,10},{2,9},{3,8},{4,15},{5,14},{6,13},{7,12},{8,3},{9,2},... | collective-permute-start | bytes 786440 | tf_op jit(solution)/shard_map/ppermute | solution.py:24
  514.0 2.9 copy-start.5
  514.0 4.0 copy-start.4
  514.0 5.2 copy-start.1
Sparse Core Ops, SparseCore 0:
  279.4 29.5 all-reduce.4
